TPU v7x, 32 devices: a whole 2x2x4 slice. The times are simulated.
32 devices in a mesh: vox: 4 (over x, core), var: 8 (over z, y).
Axes of the slice: x: 2, y: 2, z: 4, core: 2. Of those that a mesh axis runs over, the one named last changes fastest.
Arguments:
- cross: float32 [16384, 24576], P('vox', 'var')
- start: float32 [32, 24576], P(None, 'var'), may hold values from -6 to 6
- levels: int32 [2, 32], replicated, may hold values from 0 to 767, as said below
Outputs:
- deflated: float32 [16384, 24576], P('vox', 'var')
- left_dirs: float32 [32, 16384], P(None, 'vox')
- right_dirs: float32 [32, 24576], P(None, 'var')
- strength: float32 [32], replicated
Inputs may be any that keep to these rules, and one draw needn't show every extreme that they name: `levels`: both 0 and 767 occur in every draw.
All inputs are finite; a program needn't handle non-finite values.
Results may differ from a plain program's by a relative error of at most 0.0003.
Values sent between devices are 32-bit elements; how exact they have to be, the bound alone decides.
A program may use at most 192 MiB of HBM per device.

v0:
```python
import math
import jax
import jax.numpy as jnp
from jax import lax
from jax.sharding import PartitionSpec as P

NV = 16384
NG = 24576
ITERS = 2
EPSILON = 1e-06
HIGH = lax.Precision.HIGHEST


def shrink(values, thresholds, mean_sq):
    level = (thresholds * jnp.sqrt(mean_sq + EPSILON))[:, None]
    return values - jnp.clip(values, -level, level)


def local_gram(shrunk):
    return lax.dot_general(
        shrunk, shrunk, (((1,), (1,)), ((), ())), precision=HIGH, preferred_element_type=jnp.float32
    )


def apply_gram(shrunk, gram, count):
    gram = gram / count + EPSILON * jnp.eye(gram.shape[0], dtype=jnp.float32)
    factor = jnp.linalg.cholesky(gram)
    return jax.scipy.linalg.solve_triangular(factor, shrunk, lower=True)


def left_update(cross, right_dirs, thresholds):
    partial_sum = lax.dot_general(
        right_dirs,
        cross,
        (((1,), (1,)), ((), ())),
        precision=HIGH,
        preferred_element_type=jnp.float32,
    )
    summed = lax.psum(partial_sum, "var")
    first_sums = lax.psum(jnp.sum(summed * summed, 1), "vox")
    shrunk = shrink(summed, thresholds, first_sums / NV)
    gram = lax.psum(local_gram(shrunk), "vox")
    return apply_gram(shrunk, gram, NV)


def right_update(cross, left_dirs, thresholds):
    partial_sum = jnp.dot(left_dirs, cross, precision=HIGH, preferred_element_type=jnp.float32)
    summed = lax.psum(partial_sum, "vox")
    first_sums = lax.psum(jnp.sum(summed * summed, 1), "var")
    shrunk = shrink(summed, thresholds, first_sums / NG)
    gram = lax.psum(local_gram(shrunk), "var")
    return apply_gram(shrunk, gram, NG)


def per_device(cross, start, levels):
    thresholds = levels.astype(jnp.float32) / 1024.0
    right_dirs = start
    left_dirs = None
    for sweep in range(ITERS):
        left_dirs = left_update(cross, right_dirs, thresholds[0])
        right_dirs = right_update(cross, left_dirs, thresholds[1])
    projected = lax.dot_general(
        right_dirs,
        cross,
        (((1,), (1,)), ((), ())),
        precision=HIGH,
        preferred_element_type=jnp.float32,
    )
    strength = lax.psum(jnp.sum(left_dirs * projected, 1), ("vox", "var")) / math.sqrt(NV * NG)
    scaled = left_dirs * (strength / math.sqrt(NV * NG))[:, None]
    removed = lax.dot_general(
        scaled,
        right_dirs,
        (((0,), (0,)), ((), ())),
        precision=HIGH,
        preferred_element_type=jnp.float32,
    )
    deflated = cross - removed
    return (deflated, left_dirs, right_dirs, strength)


def solution(mesh):
    in_specs = (P("vox", "var"), P(None, "var"), P())
    out_specs = (P("vox", "var"), P(None, "vox"), P(None, "var"), P())
    return jax.shard_map(
        per_device, mesh=mesh, in_specs=in_specs, out_specs=out_specs, check_vma=False
    )
```

profile of v0, /device:TPU:10, one launch (start us, length us, event | category | flops | bytes accessed | tf_op | source)
XLA Modules:
  0.0 713.7 jit_solution(12268424818224196377)
XLA Ops:
  7.2 0.0 copy-start
  7.2 0.0 all-reduce.5.cloned.1.call-start
  7.2 0.9 copy-done
  8.2 49.4 %fusion.47 = f32[32,4096]{1,0:T(8,128)} fusion(f32[32,3072]{1,0:T(8,128)S(1)} %copy-done, f32[4096,3072]{1,0:T(8,128)} %param.8), kind=kOutput, calls=%fused_computation.85 | convolution fusion | flops 4831838208 | bytes 51249152 | tf_op jit(solution)/shard_map/dot_general | solution.py:32
  57.6 0.0 all-reduce.5.cloned.1.call-update
  57.6 0.0 all-reduce.7.cloned.1.call-start
  57.7 73.3 %all-reduce.5.cloned.1.call-done = f32[32,4096]{1,0:T(8,128)} async-done(((f32[32,4096]{1,0:T(8,128)}), f32[32,4096]{1,0:T(8,128)}) %all-reduce.5.cloned.1.call-update) | async-done | bytes 524304 | tf_op jit(solution)/shard_map/psum | solution.py:39
  130.9 1.2 multiply_reduce_fusion.1
  132.1 5.9 psum.92
  138.1 1.9 fusion.3
  140.0 10.7 %psum.93 = f32[32,32]{0,1:T(8,128)S(1)} all-reduce(f32[32,32]{0,1:T(8,128)S(1)} %fusion.3), channel_id=1, replica_groups=mesh['vox'=4,'var'=8] {'vox'}, use_global_device_ids=true, to_apply=%region_3.4 | all-reduce | flops 1024 | bytes 8192 | tf_op jit(solution)/shard_map/psum | solution.py:42
  150.7 0.1 copy.8
  150.8 2.9 cholesky.74
  153.7 0.6 compare_reduce_fusion.3
  154.4 0.7 fusion.27
  155.0 2.4 custom-call.10
  157.5 1.7 fusion.2
  159.2 34.2 %fusion.48 = f32[32,3072]{1,0:T(8,128)} fusion(f32[32,4096]{1,0:T(8,128)S(1)} %fusion.2, f32[4096,3072]{1,0:T(8,128)} %param.8), kind=kOutput, calls=%fused_computation.86 | convolution fusion | flops 4831838208 | bytes 51249152 | tf_op jit(solution)/shard_map/dot_general | solution.py:47
  193.4 0.0 all-reduce.7.cloned.1.call-update
  193.4 0.0 all-reduce.9.cloned.1.call-start
  193.5 31.8 %all-reduce.7.cloned.1.call-done = f32[32,3072]{1,0:T(8,128)} async-done(((f32[32,3072]{1,0:T(8,128)}), f32[32,3072]{1,0:T(8,128)}) %all-reduce.7.cloned.1.call-update) | async-done | bytes 393232 | tf_op jit(solution)/shard_map/psum | solution.py:48
  225.3 1.1 multiply_reduce_fusion.3
  226.4 18.6 %psum.95 = f32[32]{0:T(128)S(1)} all-reduce(f32[32]{0:T(128)S(1)} %multiply_reduce_fusion.3), channel_id=1, replica_groups=mesh['vox'=4,'var'=8] {'var'}, use_global_device_ids=true, to_apply=%region_8.11 | all-reduce | flops 32 | bytes 256 | tf_op jit(solution)/shard_map/psum | solution.py:49
  245.1 1.7 fusion.7
  246.8 33.2 %psum.96 = f32[32,32]{0,1:T(8,128)S(1)} all-reduce(f32[32,32]{0,1:T(8,128)S(1)} %fusion.7), channel_id=1, replica_groups=mesh['vox'=4,'var'=8] {'var'}, use_global_device_ids=true, to_apply=%region_9.12 | all-reduce | flops 1024 | bytes 8192 | tf_op jit(solution)/shard_map/psum | solution.py:51
  279.9 0.1 copy.10
  280.0 2.9 cholesky.85
  283.0 0.6 compare_reduce_fusion.2
  283.6 0.7 fusion.28
  284.3 2.4 custom-call.11
  286.7 1.6 fusion.6
  288.3 49.4 %fusion.49 = f32[32,4096]{1,0:T(8,128)} fusion(f32[32,3072]{1,0:T(8,128)S(1)} %fusion.6, f32[4096,3072]{1,0:T(8,128)} %param.8), kind=kOutput, calls=%fused_computation.87 | convolution fusion | flops 4831838208 | bytes 51249152 | tf_op jit(solution)/shard_map/dot_general | solution.py:32
  337.7 0.0 all-reduce.9.cloned.1.call-update
  337.7 0.0 all-reduce.11.cloned.1.call-start
  337.8 72.1 %all-reduce.9.cloned.1.call-done = f32[32,4096]{1,0:T(8,128)} async-done(((f32[32,4096]{1,0:T(8,128)}), f32[32,4096]{1,0:T(8,128)}) %all-reduce.9.cloned.1.call-update) | async-done | bytes 524304 | tf_op jit(solution)/shard_map/psum | solution.py:39
  409.9 1.2 multiply_reduce_fusion
  411.1 5.9 psum.98
  417.0 1.9 fusion.5
  419.0 10.4 %psum.99 = f32[32,32]{0,1:T(8,128)S(1)} all-reduce(f32[32,32]{0,1:T(8,128)S(1)} %fusion.5), channel_id=1, replica_groups=mesh['vox'=4,'var'=8] {'vox'}, use_global_device_ids=true, to_apply=%region_13.17 | all-reduce | flops 1024 | bytes 8192 | tf_op jit(solution)/shard_map/psum | solution.py:42
  429.4 0.1 copy.12
  429.4 2.9 cholesky.96
  432.4 0.6 compare_reduce_fusion.1
  433.0 0.7 fusion.29
  433.7 2.4 custom-call.12
  436.1 1.7 fusion.4
  437.9 0.0 copy-start.2
  437.9 34.4 %fusion.50 = f32[32,3072]{1,0:T(8,128)} fusion(f32[32,4096]{1,0:T(8,128)S(1)} %fusion.4, f32[4096,3072]{1,0:T(8,128)} %param.8), kind=kOutput, calls=%fused_computation.88 | convolution fusion | flops 4831838208 | bytes 51249152 | tf_op jit(solution)/shard_map/dot_general | solution.py:47
  472.3 0.0 all-reduce.11.cloned.1.call-update
  472.3 31.8 %all-reduce.11.cloned.1.call-done = f32[32,3072]{1,0:T(8,128)} async-done(((f32[32,3072]{1,0:T(8,128)}), f32[32,3072]{1,0:T(8,128)}) %all-reduce.11.cloned.1.call-update) | async-done | bytes 393232 | tf_op jit(solution)/shard_map/psum | solution.py:48
  504.1 1.1 multiply_reduce_fusion.2
  505.3 18.6 %psum.101 = f32[32]{0:T(128)S(1)} all-reduce(f32[32]{0:T(128)S(1)} %multiply_reduce_fusion.2), channel_id=1, replica_groups=mesh['vox'=4,'var'=8] {'var'}, use_global_device_ids=true, to_apply=%region_16.20 | all-reduce | flops 32 | bytes 256 | tf_op jit(solution)/shard_map/psum | solution.py:49
  523.9 1.7 fusion.9
  525.6 33.2 %psum.102 = f32[32,32]{0,1:T(8,128)S(1)} all-reduce(f32[32,32]{0,1:T(8,128)S(1)} %fusion.9), channel_id=1, replica_groups=mesh['vox'=4,'var'=8] {'var'}, use_global_device_ids=true, to_apply=%region_17.21 | all-reduce | flops 1024 | bytes 8192 | tf_op jit(solution)/shard_map/psum | solution.py:51
  558.9 0.1 copy.14
  559.0 2.9 cholesky.107
  561.9 0.6 compare_reduce_fusion
  562.6 0.7 fusion.30
  563.2 2.4 custom-call.13
  565.6 1.6 fusion.8
  567.2 0.0 copy-start.3
  567.2 48.9 %fusion = f32[32]{0:T(128)S(1)} fusion(f32[32,4096]{1,0:T(8,128)S(1)} %fusion.4, f32[32,3072]{1,0:T(8,128)S(1)} %fusion.8, f32[4096,3072]{1,0:T(8,128)} %param.8), kind=kOutput, calls=%fused_computation.2 | convolution fusion | flops 4832100352 | bytes 51249280 | tf_op jit(solution)/shard_map/dot_general | solution.py:62
  616.1 43.0 %psum.103 = f32[32]{0:T(128)S(1)} all-reduce(f32[32]{0:T(128)S(1)} %fusion), channel_id=1, replica_groups=mesh['vox'=4,'var'=8] {'vox','var'}, use_global_device_ids=true, to_apply=%region_19.23 | all-reduce | flops 32 | bytes 256 | tf_op jit(solution)/shard_map/psum | solution.py:69
  659.1 0.5 broadcast_multiply_fusion
  659.7 47.0 %convolution_subtract_fusion = f32[4096,3072]{1,0:T(8,128)} fusion(f32[4096,3072]{1,0:T(8,128)} %param.8, f32[32,3072]{1,0:T(8,128)S(1)} %fusion.8, f32[32,4096]{1,0:T(8,128)S(1)} %fusion.4, f32[32]{0:T(128)S(1)} %get-tuple-element.16), kind=kOutput, calls=%fused_computation | convolution fusion | flops 4844552192 | bytes 101580928 | tf_op jit(solution)/shard_map/dot_general | solution.py:71
  (23 shorter events, 0.3 us)
Async XLA Ops:
  7.2 1.0 copy-start
  7.2 50.5 %copy-start.4 = (s32[2,32]{1,0:T(2,128)S(1)}, s32[2,32]{1,0:T(2,128)}, u32[]{:S(2)}) copy-start(s32[2,32]{1,0:T(2,128)} %param.10) | copy-start | bytes 772
  7.2 123.8 %all-reduce.5.cloned.1.call-start = ((), (), s32[]{:S(2)}) async-start(), calls=%async_computation | async-start | bytes 1048576 | tf_op jit(solution)/shard_map/psum | solution.py:39
  57.6 167.7 %all-reduce.7.cloned.1.call-start = ((), (), s32[]{:S(2)}) async-start(), calls=%async_computation.1 | async-start | bytes 786432 | tf_op jit(solution)/shard_map/psum | solution.py:48
  193.4 216.5 %all-reduce.9.cloned.1.call-start = ((), (), s32[]{:S(2)}) async-start(), calls=%async_computation.2 | async-start | bytes 1048576 | tf_op jit(solution)/shard_map/psum | solution.py:39
  337.7 166.4 %all-reduce.11.cloned.1.call-start = ((), (), s32[]{:S(2)}) async-start(), calls=%async_computation.3 | async-start | bytes 786432 | tf_op jit(solution)/shard_map/psum | solution.py:48
  437.9 221.8 %copy-start.2 = (f32[32,4096]{1,0:T(8,128)}, f32[32,4096]{1,0:T(8,128)S(1)}, u32[]{:S(2)}) copy-start(f32[32,4096]{1,0:T(8,128)S(1)} %fusion.4) | copy-start | bytes 1572868
  567.2 139.4 %copy-start.3 = (f32[32,3072]{1,0:T(8,128)}, f32[32,3072]{1,0:T(8,128)S(1)}, u32[]{:S(2)}) copy-start(f32[32,3072]{1,0:T(8,128)S(1)} %fusion.8) | copy-start | bytes 1179652
  659.7 47.0 %copy-start.1 = (f32[32,3072]{1,0:T(8,128)S(1)}, f32[32,3072]{1,0:T(8,128)}, u32[]{:S(2)}) copy-start(f32[32,3072]{1,0:T(8,128)} %param.9) | copy-start | bytes 1179652
Sparse Core Ops, SparseCore 0:
  57.7 73.1 all-reduce.4
  193.6 31.6 all-reduce.6
  337.9 72.0 all-reduce.8
  472.4 31.6 all-reduce.10
where the time goes:
time: 720 us; the launch traced here: 714 us
  matrix products  277 us (38%)
  waiting for transfers between devices  209 us (29%)
  blocking collectives  180 us (25%)
  other arithmetic  32 us (4%)
  between operations  14.5 us (2%)
    psum x2, waiting for transfers between devices, left_update(): summed = lax.psum(partial_sum, 'var')  145 us
    dot_general x2, matrix products, left_update(): lax.dot_general(right_dirs, cross, (((1,), (1,)), ((), ())), precision=HI...  98.8 us
    dot_general x2, matrix products, right_update(): jnp.dot(left_dirs, cross, precision=HIGH, preferred_element_type=jnp.floa...  68.6 us
    psum x2, blocking collectives, right_update(): gram = lax.psum(local_gram(shrunk), 'var')  66.4 us
    psum x2, waiting for transfers between devices, right_update(): summed = lax.psum(partial_sum, 'vox')  63.6 us
    dot_general x1, matrix products, per_device(): lax.dot_general(right_dirs, cross, (((1,), (1,)), ((), ())), precision=HI...  48.9 us
    dot_general x1, matrix products, per_device(): lax.dot_general(scaled, right_dirs, (((0,), (0,)), ((), ())), precision=H...  47 us
    psum x1, blocking collectives, per_device(): lax.psum(jnp.sum(left_dirs * projected, 1), ('vox', 'var'))  43 us
  transfers between devices with their start and end apart: 4, of which 4 were waited for; matrix products, arithmetic and copies ran while one was open for 0% of the time, Pallas kernels for 0%

commit v1 on v0

--- a/solution.py
+++ b/solution.py
@@ -45,7 +45,9 @@
 
 def right_update(cross, left_dirs, thresholds):
     partial_sum = jnp.dot(left_dirs, cross, precision=HIGH, preferred_element_type=jnp.float32)
-    summed = lax.psum(partial_sum, "vox")
+    summed = partial_sum
+    for hop in (1, 2):
+        summed = summed + lax.ppermute(summed, "vox", [(dev, dev ^ hop) for dev in range(4)])
     first_sums = lax.psum(jnp.sum(summed * summed, 1), "var")
     shrunk = shrink(summed, thresholds, first_sums / NG)
     gram = lax.psum(local_gram(shrunk), "var")

time: 720 us -> 670 us (0.931)
  waiting for transfers between devices: 209 us -> 169 us
  matrix products: 277 us -> 269 us
    psum x2 -> x0, waiting for transfers between devices: 63.6 us -> none  [right_update(): summed = lax.psum(partial_sum, 'vox')]
    ppermute x0 -> x4, waiting for transfers between devices: none -> 23.4 us  [right_update(): lax.ppermute(summed, 'vox', [(dev, dev ^ hop) for dev in range(4)])]
  transfers between devices with their start and end apart: 4 -> 6, of which waited for: 4 -> 6; matrix products, arithmetic and copies ran while one was open for 0% -> 0% of each run, Pallas kernels for 0% -> 0%
where the time goes in v1:
time: 670 us; the launch traced here: 664 us
  matrix products  269 us (40%)
  blocking collectives  177 us (26%)
  waiting for transfers between devices  169 us (25%)
  other arithmetic  30.2 us (5%)
  between operations  14.5 us (2%)
    psum x2, waiting for transfers between devices, left_update(): summed = lax.psum(partial_sum, 'var')  145 us
    dot_general x2, matrix products, left_update(): lax.dot_general(right_dirs, cross, (((1,), (1,)), ((), ())), precision=HI...  98.9 us
    psum x2, blocking collectives, right_update(): gram = lax.psum(local_gram(shrunk), 'var')  66.5 us
    dot_general x2, matrix products, right_update(): jnp.dot(left_dirs, cross, precision=HIGH, preferred_element_type=jnp.floa...  65.1 us
    dot_general x1, matrix products, per_device(): lax.dot_general(right_dirs, cross, (((1,), (1,)), ((), ())), precision=HI...  48.9 us
    dot_general x1, matrix products, per_device(): lax.dot_general(scaled, right_dirs, (((0,), (0,)), ((), ())), precision=H...  47 us
    psum x1, blocking collectives, per_device(): lax.psum(jnp.sum(left_dirs * projected, 1), ('vox', 'var'))  42.5 us
    psum x2, blocking collectives, right_update(): first_sums = lax.psum(jnp.sum(summed * summed, 1), 'var')  35.1 us
  transfers between devices with their start and end apart: 6, of which 6 were waited for; matrix products, arithmetic and copies ran while one was open for 0% of the time, Pallas kernels for 0%

profile of v1, /device:TPU:10, one launch (start us, length us, event | category | flops | bytes accessed | tf_op | source)
XLA Modules:
  0.0 664.1 jit_solution(1946808345579415519)
XLA Ops:
  7.2 0.0 all-reduce.3.cloned.1.call-start
  7.2 0.9 copy-done
  8.2 49.4 %fusion.47 = f32[32,4096]{1,0:T(8,128)} fusion(f32[32,3072]{1,0:T(8,128)S(1)} %copy-done, f32[4096,3072]{1,0:T(8,128)} %param.8), kind=kOutput, calls=%fused_computation.85 | convolution fusion | flops 4831838208 | bytes 51249152 | tf_op jit(solution)/shard_map/dot_general | solution.py:32
  57.6 0.0 all-reduce.5.cloned.1.call-start
  57.7 73.3 %all-reduce.3.cloned.1.call-done = f32[32,4096]{1,0:T(8,128)} async-done(((f32[32,4096]{1,0:T(8,128)}), f32[32,4096]{1,0:T(8,128)}) %all-reduce.3.cloned.1.call-update) | async-done | bytes 524304 | tf_op jit(solution)/shard_map/psum | solution.py:39
  130.9 1.2 multiply_reduce_fusion.1
  132.1 5.9 psum.78
  138.1 1.9 fusion.3
  140.0 10.5 %psum.79 = f32[32,32]{0,1:T(8,128)S(1)} all-reduce(f32[32,32]{0,1:T(8,128)S(1)} %fusion.3), channel_id=1, replica_groups=mesh['vox'=4,'var'=8] {'vox'}, use_global_device_ids=true, to_apply=%region_3.4 | all-reduce | flops 1024 | bytes 8192 | tf_op jit(solution)/shard_map/psum | solution.py:42
  150.5 0.1 copy.8
  150.6 2.9 cholesky.74
  153.5 0.6 compare_reduce_fusion.3
  154.1 0.7 fusion.27
  154.8 2.4 custom-call.10
  157.2 1.7 fusion.2
  159.0 32.4 %fusion.48 = f32[32,3072]{1,0:T(8,128)S(1)} fusion(f32[32,4096]{1,0:T(8,128)S(1)} %fusion.2, f32[4096,3072]{1,0:T(8,128)} %param.8), kind=kOutput, calls=%fused_computation.86 | convolution fusion | flops 4831838208 | bytes 51249152 | tf_op jit(solution)/shard_map/dot_general | solution.py:47
  191.4 0.1 collective-permute-start
  191.5 1.7 collective-permute-done
  193.2 0.1 add.71
  193.3 1.2 collective-permute-start.1
  194.5 10.0 %collective-permute-done.1 = f32[32,3072]{1,0:T(8,128)S(1)} collective-permute-done((f32[32,3072]{1,0:T(8,128)S(1)}, f32[32,3072]{1,0:T(8,128)S(1)}, u32[]{:S(2)}, u32[]{:S(2)}) %collective-permute-start.1) | collective-permute-done | bytes 393248 | tf_op jit(solution)/shard_map/ppermute | solution.py:50
  204.5 0.2 multiply_reduce_fusion.3
  204.6 17.6 %psum.80 = f32[32]{0:T(128)S(1)} all-reduce(f32[32]{0:T(128)S(1)} %get-tuple-element.15), channel_id=1, replica_groups=mesh['vox'=4,'var'=8] {'var'}, use_global_device_ids=true, to_apply=%region_7.10 | all-reduce | flops 32 | bytes 256 | tf_op jit(solution)/shard_map/psum | solution.py:51
  222.2 0.6 fusion.7
  222.8 33.3 %psum.81 = f32[32,32]{0,1:T(8,128)S(1)} all-reduce(f32[32,32]{0,1:T(8,128)S(1)} %fusion.7), channel_id=1, replica_groups=mesh['vox'=4,'var'=8] {'var'}, use_global_device_ids=true, to_apply=%region_8.11 | all-reduce | flops 1024 | bytes 8192 | tf_op jit(solution)/shard_map/psum | solution.py:53
  256.2 0.1 copy.10
  256.3 2.9 cholesky.85
  259.2 0.6 compare_reduce_fusion.2
  259.8 0.7 fusion.28
  260.5 2.4 custom-call.11
  262.9 0.6 fusion.6
  263.5 49.4 %fusion.49 = f32[32,4096]{1,0:T(8,128)} fusion(f32[32,3072]{1,0:T(8,128)S(1)} %fusion.6, f32[4096,3072]{1,0:T(8,128)} %param.8), kind=kOutput, calls=%fused_computation.87 | convolution fusion | flops 4831838208 | bytes 51249152 | tf_op jit(solution)/shard_map/dot_general | solution.py:32
  313.0 0.0 all-reduce.5.cloned.1.call-update
  313.0 72.2 %all-reduce.5.cloned.1.call-done = f32[32,4096]{1,0:T(8,128)} async-done(((f32[32,4096]{1,0:T(8,128)}), f32[32,4096]{1,0:T(8,128)}) %all-reduce.5.cloned.1.call-update) | async-done | bytes 524304 | tf_op jit(solution)/shard_map/psum | solution.py:39
  385.2 1.2 multiply_reduce_fusion
  386.4 5.9 psum.83
  392.3 1.9 fusion.5
  394.2 10.8 %psum.84 = f32[32,32]{0,1:T(8,128)S(1)} all-reduce(f32[32,32]{0,1:T(8,128)S(1)} %fusion.5), channel_id=1, replica_groups=mesh['vox'=4,'var'=8] {'vox'}, use_global_device_ids=true, to_apply=%region_12.16 | all-reduce | flops 1024 | bytes 8192 | tf_op jit(solution)/shard_map/psum | solution.py:42
  405.0 0.1 copy.12
  405.1 2.9 cholesky.96
  408.0 0.6 compare_reduce_fusion.1
  408.7 0.7 fusion.29
  409.3 2.4 custom-call.12
  411.8 1.7 fusion.4
  413.5 32.6 %fusion.50 = f32[32,3072]{1,0:T(8,128)S(1)} fusion(f32[32,4096]{1,0:T(8,128)S(1)} %fusion.4, f32[4096,3072]{1,0:T(8,128)} %param.8), kind=kOutput, calls=%fused_computation.88 | convolution fusion | flops 4831838208 | bytes 51249152 | tf_op jit(solution)/shard_map/dot_general | solution.py:47
  446.1 0.1 collective-permute-start.2
  446.2 1.7 collective-permute-done.2
  447.9 0.1 add.77
  448.0 1.2 collective-permute-start.3
  449.2 10.0 %collective-permute-done.3 = f32[32,3072]{1,0:T(8,128)S(1)} collective-permute-done((f32[32,3072]{1,0:T(8,128)S(1)}, f32[32,3072]{1,0:T(8,128)S(1)}, u32[]{:S(2)}, u32[]{:S(2)}) %collective-permute-start.3) | collective-permute-done | bytes 393248 | tf_op jit(solution)/shard_map/ppermute | solution.py:50
  459.2 0.2 multiply_reduce_fusion.2
  459.4 17.6 %psum.85 = f32[32]{0:T(128)S(1)} all-reduce(f32[32]{0:T(128)S(1)} %get-tuple-element.9), channel_id=1, replica_groups=mesh['vox'=4,'var'=8] {'var'}, use_global_device_ids=true, to_apply=%region_14.18 | all-reduce | flops 32 | bytes 256 | tf_op jit(solution)/shard_map/psum | solution.py:51
  476.9 0.6 fusion.9
  477.6 33.2 %psum.86 = f32[32,32]{0,1:T(8,128)S(1)} all-reduce(f32[32,32]{0,1:T(8,128)S(1)} %fusion.9), channel_id=1, replica_groups=mesh['vox'=4,'var'=8] {'var'}, use_global_device_ids=true, to_apply=%region_15.19 | all-reduce | flops 1024 | bytes 8192 | tf_op jit(solution)/shard_map/psum | solution.py:53
  510.7 0.1 copy.14
  510.8 2.9 cholesky.107
  513.8 0.6 compare_reduce_fusion
  514.4 0.7 fusion.30
  515.1 2.4 custom-call.13
  517.5 0.6 fusion.8
  518.1 48.9 %fusion = f32[32]{0:T(128)S(1)} fusion(f32[32,4096]{1,0:T(8,128)S(1)} %fusion.4, f32[32,3072]{1,0:T(8,128)S(1)} %fusion.8, f32[4096,3072]{1,0:T(8,128)} %param.8), kind=kOutput, calls=%fused_computation.2 | convolution fusion | flops 4832100352 | bytes 51249280 | tf_op jit(solution)/shard_map/dot_general | solution.py:64
  567.0 42.5 %psum.87 = f32[32]{0:T(128)S(1)} all-reduce(f32[32]{0:T(128)S(1)} %fusion), channel_id=1, replica_groups=mesh['vox'=4,'var'=8] {'vox','var'}, use_global_device_ids=true, to_apply=%region_17.21 | all-reduce | flops 32 | bytes 256 | tf_op jit(solution)/shard_map/psum | solution.py:71
  609.5 0.5 broadcast_multiply_fusion
  610.1 47.0 %convolution_subtract_fusion = f32[4096,3072]{1,0:T(8,128)} fusion(f32[4096,3072]{1,0:T(8,128)} %param.8, f32[32,3072]{1,0:T(8,128)S(1)} %fusion.8, f32[32,4096]{1,0:T(8,128)S(1)} %fusion.4, f32[32]{0:T(128)S(1)} %get-tuple-element.20), kind=kOutput, calls=%fused_computation | convolution fusion | flops 4844552192 | bytes 101580928 | tf_op jit(solution)/shard_map/dot_general | solution.py:73
  (27 shorter events, 0.3 us)
Async XLA Ops:
  7.2 1.0 copy-start
  7.2 50.5 %copy-start.4 = (s32[2,32]{1,0:T(2,128)S(1)}, s32[2,32]{1,0:T(2,128)}, u32[]{:S(2)}) copy-start(s32[2,32]{1,0:T(2,128)} %param.10) | copy-start | bytes 772
  7.2 123.8 %all-reduce.3.cloned.1.call-start = ((), (), s32[]{:S(2)}) async-start(), calls=%async_computation | async-start | bytes 1048576 | tf_op jit(solution)/shard_map/psum | solution.py:39
  57.6 327.6 %all-reduce.5.cloned.1.call-start = ((), (), s32[]{:S(2)}) async-start(), calls=%async_computation.1 | async-start | bytes 1048576 | tf_op jit(solution)/shard_map/psum | solution.py:39
  191.4 1.8 collective-permute-start
  193.3 11.2 %collective-permute-start.1 = (f32[32,3072]{1,0:T(8,128)S(1)}, f32[32,3072]{1,0:T(8,128)S(1)}, u32[]{:S(2)}, u32[]{:S(2)}) collective-permute-start(f32[32,3072]{1,0:T(8,128)S(1)} %add.71), channel_id=1, source_target_pairs={{0,16},{8,24},{16,0},{24,8},{1,17},{9,25},{17,1},{25,9},{2,18},{10... | collective-permute-start | bytes 1179656 | tf_op jit(solution)/shard_map/ppermute | solution.py:50
  413.5 196.6 %copy-start.2 = (f32[32,4096]{1,0:T(8,128)}, f32[32,4096]{1,0:T(8,128)S(1)}, u32[]{:S(2)}) copy-start(f32[32,4096]{1,0:T(8,128)S(1)} %fusion.4) | copy-start | bytes 1572868
  446.1 1.8 collective-permute-start.2
  448.0 11.2 %collective-permute-start.3 = (f32[32,3072]{1,0:T(8,128)S(1)}, f32[32,3072]{1,0:T(8,128)S(1)}, u32[]{:S(2)}, u32[]{:S(2)}) collective-permute-start(f32[32,3072]{1,0:T(8,128)S(1)} %add.77), channel_id=1, source_target_pairs={{0,16},{8,24},{16,0},{24,8},{1,17},{9,25},{17,1},{25,9},{2,18},{10... | collective-permute-start | bytes 1179656 | tf_op jit(solution)/shard_map/ppermute | solution.py:50
  518.1 138.9 %copy-start.3 = (f32[32,3072]{1,0:T(8,128)}, f32[32,3072]{1,0:T(8,128)S(1)}, u32[]{:S(2)}) copy-start(f32[32,3072]{1,0:T(8,128)S(1)} %fusion.8) | copy-start | bytes 1179652
  610.1 47.0 %copy-start.1 = (f32[32,3072]{1,0:T(8,128)S(1)}, f32[32,3072]{1,0:T(8,128)}, u32[]{:S(2)}) copy-start(f32[32,3072]{1,0:T(8,128)} %param.9) | copy-start | bytes 1179652
Sparse Core Ops, SparseCore 0:
  57.7 73.1 all-reduce.2
  313.1 72.0 all-reduce.4
